TPU v7x, 256 devices: a whole 4x4x8 slice. The times are simulated.
256 devices in a mesh: replica: 8 (over x, core), outer: 4 (over y), link: 8 (over z).
Axes of the slice: x: 4, y: 4, z: 8, core: 2. Of those that a mesh axis runs over, the one named last changes fastest.
Arguments:
- link_in: bfloat16 [8, 16384, 256], P('replica', ('outer', 'link')), may hold values from -6 to 6
- path_in: bfloat16 [8, 4096, 256], P('replica', ('outer', 'link')), may hold values from -6 to 6
- hop_slots: int32 [8, 4096, 24], P('replica', ('outer', 'link')), may hold values from 0 to 2047
- hop_lens: int32 [8, 4096], P('replica', ('outer', 'link')), may hold values from 2 to 24
- failed: int32 [8, 16384], P('replica', ('outer', 'link')), may hold values 0 or 1
- serve_index: int32 [8, 32, 32, 64], P('replica', None, ('outer', 'link')), may hold values from 0 to 511
- link_grad: bfloat16 [8, 16384, 256], P('replica', ('outer', 'link')), may hold values from -6 to 6
- path_grad: bfloat16 [8, 4096, 256], P('replica', ('outer', 'link')), may hold values from -6 to 6
- gru_wx: bfloat16 [256, 768], replicated, may hold values from -0.375 to 0.375
- gru_wh: bfloat16 [256, 768], replicated, may hold values from -0.375 to 0.375
- gru_bias: float32 [768], replicated, may hold values from -3 to 3
- mlp_w1: bfloat16 [512, 256], replicated, may hold values from -0.25 to 0.25
- mlp_b1: float32 [256], replicated, may hold values from -3 to 3
- mlp_w2: bfloat16 [256, 256], replicated, may hold values from -0.375 to 0.375
- mlp_b2: float32 [256], replicated, may hold values from -3 to 3
Outputs:
- link_out: bfloat16 [8, 16384, 256], P('replica', ('outer', 'link'))
- path_out: bfloat16 [8, 4096, 256], P('replica', ('outer', 'link'))
- link_in_grad: float32 [8, 16384, 256], P('replica', ('outer', 'link'))
- path_in_grad: float32 [8, 4096, 256], P('replica', ('outer', 'link'))
- grad_wx: float32 [256, 768], replicated
- grad_wh: float32 [256, 768], replicated
- grad_bias: float32 [768], replicated
- grad_w1: float32 [512, 256], replicated
- grad_b1: float32 [256], replicated
- grad_w2: float32 [256, 256], replicated
- grad_b2: float32 [256], replicated
Inputs may be any that keep to these rules, and one draw needn't show every extreme that they name: `serve_index`: entry [s, d, o, c] names, among the 512 links of owner device o, the link in request slot c of device d; a link may fill several slots. `hop_slots`: slot o * 64 + c is request slot c of the flow's own device towards owner o; entries at hops past the flow's length are ignored. 1 marks a failed link.
All inputs are finite; a program needn't handle non-finite values. No bound on the sum of `failed` on one device may be relied on, other than what follows from the above.
Results may differ from a plain program's by a relative error of at most 0.0067.
Values may be sent and summed in bfloat16 or wider, within the bound.
No kernel may reach another device: no remote copies, remote signals or barrier semaphores. Data moves between devices by JAX's collectives and lax.ppermute only.
A program may use at most 128 MiB of HBM per device.

v0:
```python
import jax
import jax.numpy as jnp
from jax import lax
from jax.sharding import PartitionSpec as P


def gate_terms(state_now, hop_input, input_weight, hidden_weight, gate_bias):
    from_input = jnp.dot(hop_input, input_weight, preferred_element_type=jnp.float32) + gate_bias
    from_state = jnp.dot(
        state_now.astype(jnp.bfloat16), hidden_weight, preferred_element_type=jnp.float32
    )
    return (from_input, from_state)


def gru_cell(state_now, from_input, from_state):
    feat_width = state_now.shape[1]
    update = jax.nn.sigmoid(from_input[:, :feat_width] + from_state[:, :feat_width])
    reset = jax.nn.sigmoid(
        from_input[:, feat_width : 2 * feat_width] + from_state[:, feat_width : 2 * feat_width]
    )
    candidate = jnp.tanh(from_input[:, 2 * feat_width :] + reset * from_state[:, 2 * feat_width :])
    return (candidate + update * (state_now - candidate), update, reset, candidate)


def gru_forward(path_start, hop_inputs, live_mask, input_weight, hidden_weight, gate_bias):

    def advance(state_now, scan_item):
        hop_input, live_now = scan_item
        from_input, from_state = gate_terms(
            state_now, hop_input, input_weight, hidden_weight, gate_bias
        )
        stepped = gru_cell(state_now, from_input, from_state)[0]
        state_next = jnp.where(live_now[:, None] > 0, stepped, state_now)
        return (state_next, (state_next,))

    return lax.scan(advance, path_start.astype(jnp.float32), (hop_inputs, live_mask))[1]


def back_step(
    carried, hop_input, state_now, live_now, hop_grad, from_input, from_state, input_tr, hidden_tr
):
    grad_state, grad_wx, grad_wh, grad_bias = carried
    feat_width = state_now.shape[1]
    live_col = live_now[:, None]
    grad_state = grad_state + live_col * hop_grad
    update, reset, candidate = gru_cell(state_now, from_input, from_state)[1:]
    pre_update = grad_state * (state_now - candidate) * update * (1.0 - update)
    pre_cand = grad_state * (1.0 - update) * (1.0 - candidate * candidate)
    pre_reset = pre_cand * from_state[:, 2 * feat_width :] * reset * (1.0 - reset)
    grad_in = jnp.concatenate([pre_update, pre_reset, pre_cand], axis=1) * live_col
    grad_hid = jnp.concatenate([pre_update, pre_reset, pre_cand * reset], axis=1) * live_col
    in_bf = grad_in.astype(jnp.bfloat16)
    hid_bf = grad_hid.astype(jnp.bfloat16)
    grad_prev = jnp.where(
        live_col > 0,
        grad_state * update + jnp.dot(hid_bf, hidden_tr, preferred_element_type=jnp.float32),
        grad_state,
    )
    grad_input = jnp.dot(in_bf, input_tr, preferred_element_type=jnp.float32)
    grad_wx = grad_wx + jnp.dot(hop_input.T, in_bf, preferred_element_type=jnp.float32)
    grad_wh = grad_wh + jnp.dot(
        state_now.astype(jnp.bfloat16).T, hid_bf, preferred_element_type=jnp.float32
    )
    grad_bias = grad_bias + jnp.sum(grad_in, axis=0)
    return ((grad_prev, grad_wx, grad_wh, grad_bias), grad_input)


def gru_backward(
    path_start,
    states,
    hop_inputs,
    live_mask,
    hop_grads,
    path_grad,
    input_weight,
    hidden_weight,
    gate_bias,
):
    feat_width = path_start.shape[1]
    prior_states = jnp.concatenate([path_start.astype(jnp.float32)[None], states[:-1]], axis=0)
    input_tr = input_weight.T
    hidden_tr = hidden_weight.T
    initial = (
        path_grad.astype(jnp.float32),
        jnp.zeros((feat_width, 3 * feat_width), jnp.float32),
        jnp.zeros((feat_width, 3 * feat_width), jnp.float32),
        jnp.zeros((3 * feat_width,), jnp.float32),
    )

    def retreat(carried, scan_item):
        hop_input, state_now, live_now, hop_grad = scan_item
        from_input, from_state = gate_terms(
            state_now, hop_input, input_weight, hidden_weight, gate_bias
        )
        return back_step(
            carried,
            hop_input,
            state_now,
            live_now,
            hop_grad,
            from_input,
            from_state,
            input_tr,
            hidden_tr,
        )

    scan_items = (hop_inputs, prior_states, live_mask, hop_grads)
    return lax.scan(retreat, initial, scan_items, reverse=True)


def link_forward(link_rows, agg_bf, keep_col, mlp_w1, mlp_b1, mlp_w2, mlp_b2):
    feat_width = link_rows.shape[1]
    pre_act = (
        jnp.dot(link_rows, mlp_w1[:feat_width], preferred_element_type=jnp.float32)
        + jnp.dot(agg_bf, mlp_w1[feat_width:], preferred_element_type=jnp.float32)
        + mlp_b1
    )
    activ = jax.nn.silu(pre_act).astype(jnp.bfloat16)
    value = (
        link_rows.astype(jnp.float32)
        + jnp.dot(activ, mlp_w2, preferred_element_type=jnp.float32)
        + mlp_b2
    )
    return ((keep_col * value).astype(jnp.bfloat16), pre_act, activ)


def link_backward(link_grad_rows, link_rows, agg_bf, keep_col, pre_act, activ, mlp_w1, mlp_w2):
    feat_width = link_rows.shape[1]
    grad_val = keep_col * link_grad_rows.astype(jnp.float32)
    val_bf = grad_val.astype(jnp.bfloat16)
    grad_w2 = jnp.dot(activ.T, val_bf, preferred_element_type=jnp.float32)
    grad_b2 = jnp.sum(grad_val, axis=0)
    grad_act = jnp.dot(val_bf, mlp_w2.T, preferred_element_type=jnp.float32)
    sigma = jax.nn.sigmoid(pre_act)
    grad_pre = grad_act * sigma * (1.0 + pre_act * (1.0 - sigma))
    pre_bf = grad_pre.astype(jnp.bfloat16)
    grad_w1 = jnp.concatenate(
        [
            jnp.dot(link_rows.T, pre_bf, preferred_element_type=jnp.float32),
            jnp.dot(agg_bf.T, pre_bf, preferred_element_type=jnp.float32),
        ],
        axis=0,
    )
    grad_b1 = jnp.sum(grad_pre, axis=0)
    link_direct = grad_val + jnp.dot(
        pre_bf, mlp_w1[:feat_width].T, preferred_element_type=jnp.float32
    )
    agg_grad = jnp.dot(pre_bf, mlp_w1[feat_width:].T, preferred_element_type=jnp.float32).astype(
        jnp.bfloat16
    )
    return (link_direct, agg_grad, (grad_w1, grad_b1, grad_w2, grad_b2))


def swap_slots(blocks):
    return lax.all_to_all(blocks, ("outer", "link"), split_axis=0, concat_axis=0, tiled=True)


def body(
    link_in,
    path_in,
    hop_slots,
    hop_lens,
    failed,
    serve_index,
    link_grad,
    path_grad,
    gru_wx,
    gru_wh,
    gru_bias,
    mlp_w1,
    mlp_b1,
    mlp_w2,
    mlp_b2,
):
    link_rows = link_in[0]
    feat_width = link_rows.shape[1]
    link_count = link_rows.shape[0]
    serve_rows = serve_index[0, :, 0, :]
    group_size, slot_cap = serve_rows.shape
    serve_flat = serve_rows.reshape(-1)
    slot_ids = hop_slots[0].T
    hop_count, flow_count = slot_ids.shape
    flat_slots = slot_ids.reshape(-1)
    live_mask = (jnp.arange(hop_count, dtype=jnp.int32)[:, None] < hop_lens[0][None, :]).astype(
        jnp.float32
    )
    fetched = swap_slots(jnp.take(link_rows, serve_rows, axis=0))
    hop_inputs = jnp.take(fetched.reshape(group_size * slot_cap, feat_width), slot_ids, axis=0)
    states = gru_forward(path_in[0], hop_inputs, live_mask, gru_wx, gru_wh, gru_bias)[0]
    partial_value = jax.ops.segment_sum(
        (states * live_mask[:, :, None]).reshape(hop_count * flow_count, feat_width),
        flat_slots,
        num_segments=group_size * slot_cap,
    ).astype(jnp.bfloat16)
    arrived = swap_slots(partial_value.reshape(group_size, slot_cap, feat_width))
    aggregate = jax.ops.segment_sum(
        arrived.reshape(group_size * slot_cap, feat_width).astype(jnp.float32),
        serve_flat,
        num_segments=link_count,
    )
    agg_bf = aggregate.astype(jnp.bfloat16)
    keep_col = (1 - failed[0]).astype(jnp.float32)[:, None]
    link_out, pre_act, activ = link_forward(
        link_rows, agg_bf, keep_col, mlp_w1, mlp_b1, mlp_w2, mlp_b2
    )
    path_out = states[-1].astype(jnp.bfloat16)
    link_direct, agg_grad, mlp_terms = link_backward(
        link_grad[0], link_rows, agg_bf, keep_col, pre_act, activ, mlp_w1, mlp_w2
    )
    returned = swap_slots(jnp.take(agg_grad, serve_rows, axis=0))
    hop_grads = (
        jnp.take(returned.reshape(group_size * slot_cap, feat_width), slot_ids, axis=0).astype(
            jnp.float32
        )
        * live_mask[:, :, None]
    )
    finished, grad_inputs = gru_backward(
        path_in[0], states, hop_inputs, live_mask, hop_grads, path_grad[0], gru_wx, gru_wh, gru_bias
    )
    dpart = jax.ops.segment_sum(
        grad_inputs.reshape(hop_count * flow_count, feat_width),
        flat_slots,
        num_segments=group_size * slot_cap,
    ).astype(jnp.bfloat16)
    owned = swap_slots(dpart.reshape(group_size, slot_cap, feat_width))
    link_back = link_direct + jax.ops.segment_sum(
        owned.reshape(group_size * slot_cap, feat_width).astype(jnp.float32),
        serve_flat,
        num_segments=link_count,
    )
    summed = lax.psum(
        (
            finished[1],
            finished[2],
            finished[3],
            mlp_terms[0],
            mlp_terms[1],
            mlp_terms[2],
            mlp_terms[3],
        ),
        ("replica", "outer", "link"),
    )
    device_count = lax.axis_size("replica") * lax.axis_size("outer") * lax.axis_size("link")
    grad_scale = float(device_count * link_count) ** (-0.5)
    return (
        link_out[None],
        path_out[None],
        link_back[None],
        finished[0][None],
        summed[0] * grad_scale,
        summed[1] * grad_scale,
        summed[2] * grad_scale,
        summed[3] * grad_scale,
        summed[4] * grad_scale,
        summed[5] * grad_scale,
        summed[6] * grad_scale,
    )


def solution(mesh):
    return jax.shard_map(
        body,
        mesh=mesh,
        in_specs=(
            P("replica", ("outer", "link"), None),
            P("replica", ("outer", "link"), None),
            P("replica", ("outer", "link"), None),
            P("replica", ("outer", "link")),
            P("replica", ("outer", "link")),
            P("replica", None, ("outer", "link"), None),
            P("replica", ("outer", "link"), None),
            P("replica", ("outer", "link"), None),
            P(),
            P(),
            P(),
            P(),
            P(),
            P(),
            P(),
        ),
        out_specs=(
            P("replica", ("outer", "link"), None),
            P("replica", ("outer", "link"), None),
            P("replica", ("outer", "link"), None),
            P("replica", ("outer", "link"), None),
            P(),
            P(),
            P(),
            P(),
            P(),
            P(),
            P(),
        ),
        check_vma=False,
    )
```

profile of v0, /device:TPU:2, one launch (start us, length us, event | category | flops | bytes accessed | tf_op | source)
XLA Modules:
  0.0 706.7 jit_solution(12861078215785412026)
XLA Ops:
  8.8 7.6 %gather_fusion = bf16[2048,256]{1,0:T(8,128)(2,1)S(1)} fusion(bf16[512,256]{1,0:T(8,128)(2,1)} %bitcast.135, s32[2048]{0:T(1024)S(1)} %broadcast_clamp_fusion), kind=kCustom, calls=%fused_computation.clone | custom fusion | bytes 2105344 | tf_op jit(solution)/shard_map/jit(_take)/gather | solution.py:187
  17.7 11.5 %all-to-all-start = ((bf16[32,64,256]{2,1,0:T(8,128)(2,1)}), bf16[32,64,256]{2,1,0:T(8,128)(2,1)S(1)}, u32[]{:S(2)}, u32[]{:S(2)}) async-start(bf16[32,64,256]{2,1,0:T(8,128)(2,1)} %broadcast_select_fusion.2), calls=%async_computation | async-start | bytes 2097152 | tf_op jit(solution)/shard_map/all_to_all | solution.py:155
  29.9 27.9 %all-to-all-done = bf16[32,64,256]{2,1,0:T(8,128)(2,1)S(1)} async-done(((bf16[32,64,256]{2,1,0:T(8,128)(2,1)}), bf16[32,64,256]{2,1,0:T(8,128)(2,1)S(1)}, u32[]{:S(2)}, u32[]{:S(2)}) %all-to-all-start) | async-done | bytes 1048608 | tf_op jit(solution)/shard_map/all_to_all | solution.py:155
  57.8 13.0 %gather_fusion.1 = bf16[3072,256]{1,0:T(8,128)(2,1)} fusion(bf16[2048,256]{1,0:T(8,128)(2,1)S(1)} %bitcast.137, s32[3072]{0:T(1024)S(1)} %bitcast_clamp_fusion), kind=kCustom, calls=%fused_computation.1.clone | custom fusion | bytes 3158016 | tf_op jit(solution)/shard_map/jit(_take)/gather | solution.py:188
  74.6 29.4 %while.35 = (s32[]{:T(128)}, f32[128,256]{1,0:T(8,128)S(1)}, f32[24,128,256]{2,1,0:T(8,128)}, f32[24,128]{1,0:T(8,128)S(1)}, bf16[24,128,256]{2,1,0:T(8,128)(2,1...) while((s32[]{:T(128)}, f32[128,256]{1,0:T(8,128)S(1)}, ...), condition=%wide.region_1.4_spmd, body=%wide.region_0.3_spmd.sunk | while | flops 101253248 | bytes 2954097 | solution.py:36
  104.0 4.6 broadcast_multiply_fusion
  108.5 17.9 %scatter_custom_fusion = f32[2048,256]{1,0:T(8,128)S(1)} fusion(s32[3072]{0:T(1024)S(1)} %bitcast.155, f32[3072,256]{1,0:T(8,128)} %bitcast.148, f32[]{:T(128)} %constant.108.clone.1), kind=kCustom, calls=%fused_computation.102 | custom fusion | flops 786432 | bytes 2097664 | tf_op jit(solution)/shard_map/scatter-add | solution.py:190
  127.6 5.2 all-to-all-start.1
  135.5 25.6 %all-to-all-done.1 = bf16[32,64,256]{2,1,0:T(8,128)(2,1)S(1)} async-done(((bf16[32,64,256]{2,1,0:T(8,128)(2,1)}), bf16[32,64,256]{2,1,0:T(8,128)(2,1)S(1)}, u32[]{:S(2)}, u32[]{:S(2)}) %all-to-all-start.1) | async-done | bytes 1048608 | tf_op jit(solution)/shard_map/all_to_all | solution.py:155
  161.1 11.9 %scatter_custom_fusion.1 = f32[512,256]{1,0:T(8,128)S(1)} fusion(s32[2048]{0:T(1024)} %reshape.174, bf16[2048,256]{1,0:T(8,128)(2,1)S(1)} %bitcast.146, f32[]{:T(128)} %constant.108.clone.1), kind=kCustom, calls=%fused_computation.84 | custom fusion | flops 1048576 | bytes 1573376 | tf_op jit(solution)/shard_map/scatter-add | solution.py:196
  173.9 2.1 fusion.85
  177.0 7.5 %gather_fusion.2 = bf16[2048,256]{1,0:T(8,128)(2,1)S(1)} fusion(bf16[512,256]{1,0:T(8,128)(2,1)S(1)} %convolution_convert_fusion, s32[2048]{0:T(1024)S(1)} %broadcast_clamp_fusion), kind=kCustom, calls=%fused_computation.2.clone | custom fusion | bytes 2105344 | tf_op jit(solution)/shard_map/jit(_take)/gather | solution.py:210
  185.7 4.9 all-to-all-start.2
  194.2 2.1 slice.91
  200.7 18.2 %all-to-all-done.2 = bf16[32,64,256]{2,1,0:T(8,128)(2,1)S(1)} async-done(((bf16[32,64,256]{2,1,0:T(8,128)(2,1)}), bf16[32,64,256]{2,1,0:T(8,128)(2,1)S(1)}, u32[]{:S(2)}, u32[]{:S(2)}) %all-to-all-start.2) | async-done | bytes 1048608 | tf_op jit(solution)/shard_map/all_to_all | solution.py:155
  218.9 12.9 %gather_fusion.3 = bf16[3072,256]{1,0:T(8,128)(2,1)} fusion(bf16[2048,256]{1,0:T(8,128)(2,1)S(1)} %bitcast.136, s32[3072]{0:T(1024)S(1)} %copy-done.32), kind=kCustom, calls=%fused_computation.3.clone | custom fusion | bytes 3158016 | tf_op jit(solution)/shard_map/jit(_take)/gather | solution.py:212
  231.9 4.1 convert_multiply_fusion
  236.0 2.1 broadcast.84
  238.1 176.1 %while.36 = (s32[]{:T(128)}, f32[128,256]{1,0:T(8,128)S(1)}, f32[256,768]{1,0:T(8,128)S(1)}, f32[256,768]{1,0:T(8,128)S(1)}, f32[768]{0:T(1024)S(1)}, /*index=5*...) while((s32[]{:T(128)}, f32[128,256]{1,0:T(8,128)S(1)}, ...), condition=%wide.region_6.9_spmd.clone, body=%wide.region_4.8_spmd.clone.sunk | while | flops 306152320 | bytes 12996093 | solution.py:108
  417.0 17.9 %scatter_custom_fusion.2 = f32[2048,256]{1,0:T(8,128)S(1)} fusion(s32[3072]{0:T(1024)} %bitcast.154, f32[3072,256]{1,0:T(8,128)} %bitcast.147, f32[]{:T(128)} %constant.108.clone.1), kind=kCustom, calls=%fused_computation.100 | custom fusion | flops 786432 | bytes 2097664 | tf_op jit(solution)/shard_map/scatter-add | solution.py:220
  436.0 5.1 all-to-all-start.3
  442.4 76.8 %all-reduce = (f32[768]{0:T(1024)S(1)}, f32[256]{0:T(256)S(1)}, f32[256]{0:T(256)S(1)}) all-reduce(f32[768]{0:T(1024)S(1)} %get-tuple-element.357, f32[256]{0:T(256)S(1)} %copy-done.39, f32[256]{0:T(256)S(1)} %fusion.64), channel_id=1, replica_groups=mesh['replica'=8,'outer'=4,'link'=8] {'replica','outer','link'}, use_global_device_ids=true, to_apply=%region_11.14 | all-reduce | flops 1280 | bytes 10240 | tf_op jit(solution)/shard_map/psum | solution.py:231
  520.9 160.5 %all-reduce.4.cloned.1.call-done = (f32[256,768]{1,0:T(8,128)}, f32[256,768]{1,0:T(8,128)}, f32[512,256]{1,0:T(8,128)}, f32[256,256]{1,0:T(8,128)}) async-done(((f32[256,768]{1,0:T(8,128)}, f32[256,768]{1,0:T(8,128)}, f32[512,256]{1,0:T(8,128)}, f32[256,256]{1,0:T(8,128)}), (f32[256,768]{1,0:T(8,128)}, f32[256,768]{1,0:T(8,128)}, f32[512,256]{1,0:T(8,128)}, ...) | async-done | bytes 2359312 | tf_op jit(solution)/shard_map/psum | solution.py:231
  687.1 12.0 %scatter_custom_fusion.3 = f32[512,256]{1,0:T(8,128)S(1)} fusion(f32[512,256]{1,0:T(8,128)S(1)} %convolution_add_fusion.5, s32[2048]{0:T(1024)} %reshape.174, bf16[2048,256]{1,0:T(8,128)(2,1)S(1)} %bitcast.145), kind=kCustom, calls=%fused_computation.82 | custom fusion | flops 1048576 | bytes 1572864 | tf_op jit(solution)/shard_map/scatter-add | solution.py:226
  (559 shorter events, 238.4 us)
Async XLA Ops:
  7.2 166.7 %copy-start = (bf16[256,256]{1,0:T(8,128)(2,1)S(1)}, bf16[256,256]{1,0:T(8,128)(2,1)}, u32[]{:S(2)}) copy-start(bf16[256,256]{1,0:T(8,128)(2,1)} %param.36) | copy-start | bytes 393220
  16.4 12.8 %copy-start.34 = (s32[1,128,24]{1,2,0:T(8,128)S(1)}, s32[1,128,24]{1,2,0:T(8,128)}, u32[]{:S(2)}) copy-start(s32[1,128,24]{1,2,0:T(8,128)} %param.25) | copy-start | bytes 36868
  16.4 12.8 %copy-start.40 = (s32[1,128]{1,0:T(1,128)S(1)}, s32[1,128]{1,0:T(1,128)}, u32[]{:S(2)}) copy-start(s32[1,128]{1,0:T(1,128)} %param.26) | copy-start | bytes 1540
  16.4 12.8 %copy-start.33 = (bf16[1,128,256]{2,1,0:T(8,128)(2,1)S(1)}, bf16[1,128,256]{2,1,0:T(8,128)(2,1)}, u32[]{:S(2)}) copy-start(bf16[1,128,256]{2,1,0:T(8,128)(2,1)} %param.24) | copy-start | bytes 196612
  17.7 40.1 %all-to-all-start = ((bf16[32,64,256]{2,1,0:T(8,128)(2,1)}), bf16[32,64,256]{2,1,0:T(8,128)(2,1)S(1)}, u32[]{:S(2)}, u32[]{:S(2)}) async-start(bf16[32,64,256]{2,1,0:T(8,128)(2,1)} %broadcast_select_fusion.2), calls=%async_computation | async-start | bytes 2097152 | tf_op jit(solution)/shard_map/all_to_all | solution.py:155
  29.2 41.6 %copy-start.31 = (s32[3072]{0:T(1024)}, s32[3072]{0:T(1024)S(1)}, u32[]{:S(2)}) copy-start(s32[3072]{0:T(1024)S(1)} %bitcast_clamp_fusion) | copy-start | bytes 36868
  29.2 41.5 %copy-start.35 = (pred[24,128]{1,0:T(8,128)(4,1)}, pred[24,128]{1,0:T(8,128)(4,1)S(1)}, u32[]{:S(2)}) copy-start(pred[24,128]{1,0:T(8,128)(4,1)S(1)} %get-tuple-element.474) | copy-start | bytes 9220
  126.5 8.8 %copy-start.1 = (bf16[1,512,256]{2,1,0:T(8,128)(2,1)S(1)}, bf16[1,512,256]{2,1,0:T(8,128)(2,1)}, u32[]{:S(2)}) copy-start(bf16[1,512,256]{2,1,0:T(8,128)(2,1)} %param.23) | copy-start | bytes 786436
  126.5 8.8 %copy-start.13 = (bf16[512,256]{1,0:T(8,128)(2,1)S(1)}, bf16[512,256]{1,0:T(8,128)(2,1)}, u32[]{:S(2)}) copy-start(bf16[512,256]{1,0:T(8,128)(2,1)} %param.34) | copy-start | bytes 786436
  127.6 5.8 copy-start.28
  127.6 7.1 %copy-start.38 = (s32[1,512]{1,0:T(1,128)S(1)}, s32[1,512]{1,0:T(1,128)}, u32[]{:S(2)}) copy-start(s32[1,512]{1,0:T(1,128)} %param.27) | copy-start | bytes 6148
  127.6 45.4 %copy-start.14 = (bf16[512,256]{1,0:T(8,128)(2,1)S(1)}, bf16[512,256]{1,0:T(8,128)(2,1)}, u32[]{:S(2)}) copy-start(bf16[512,256]{1,0:T(8,128)(2,1)} %param.34) | copy-start | bytes 786436
  127.6 33.5 %all-to-all-start.1 = ((bf16[32,64,256]{2,1,0:T(8,128)(2,1)}), bf16[32,64,256]{2,1,0:T(8,128)(2,1)S(1)}, u32[]{:S(2)}, u32[]{:S(2)}) async-start(bf16[32,64,256]{2,1,0:T(8,128)(2,1)} %bitcast.142), calls=%async_computation.1 | async-start | bytes 2097152 | tf_op jit(solution)/shard_map/all_to_all | solution.py:155
  185.7 33.2 %all-to-all-start.2 = ((bf16[32,64,256]{2,1,0:T(8,128)(2,1)}), bf16[32,64,256]{2,1,0:T(8,128)(2,1)S(1)}, u32[]{:S(2)}, u32[]{:S(2)}) async-start(bf16[32,64,256]{2,1,0:T(8,128)(2,1)} %broadcast_select_fusion.1), calls=%async_computation.2 | async-start | bytes 2097152 | tf_op jit(solution)/shard_map/all_to_all | solution.py:155
  190.6 490.8 %all-reduce.4.cloned.1.call-start = ((), (), s32[]{:S(2)}) async-start(), calls=%async_computation.4 | async-start | bytes 4718592 | tf_op jit(solution)/shard_map/psum | solution.py:231
  198.8 20.2 %copy-start.32 = (s32[3072]{0:T(1024)S(1)}, s32[3072]{0:T(1024)}, u32[]{:S(2)}) copy-start(s32[3072]{0:T(1024)} %copy-done.31) | copy-start | bytes 36868
  218.9 12.9 %copy-start.30 = (f32[24,128]{1,0:T(8,128)S(1)}, f32[24,128]{1,0:T(8,128)}, u32[]{:S(2)}) copy-start(f32[24,128]{1,0:T(8,128)} %copy-done.29) | copy-start | bytes 36868
  218.9 13.0 %copy-start.36 = (pred[24,128]{1,0:T(8,128)(4,1)S(1)}, pred[24,128]{1,0:T(8,128)(4,1)}, u32[]{:S(2)}) copy-start(pred[24,128]{1,0:T(8,128)(4,1)} %copy-done.35) | copy-start | bytes 9220
  414.1 20.8 %copy-start.8 = (f32[128,256]{1,0:T(8,128)}, f32[128,256]{1,0:T(8,128)S(1)}, u32[]{:S(2)}) copy-start(f32[128,256]{1,0:T(8,128)S(1)} %get-tuple-element.354) | copy-start | bytes 393220
  434.9 6.2 copy-start.41
  436.0 5.1 copy-start.22
  436.0 6.1 copy-start.11
  436.0 6.1 copy-start.15
  436.0 251.0 %all-to-all-start.3 = ((bf16[32,64,256]{2,1,0:T(8,128)(2,1)}), bf16[32,64,256]{2,1,0:T(8,128)(2,1)S(1)}, u32[]{:S(2)}, u32[]{:S(2)}) async-start(bf16[32,64,256]{2,1,0:T(8,128)(2,1)} %bitcast.141), calls=%async_computation.3 | async-start | bytes 2097152 | tf_op jit(solution)/shard_map/all_to_all | solution.py:155
  (46 other events, 102.7 us)
Sparse Core Ops, SparseCore 0:
  415.4 265.9 all-reduce.3
where the time goes:
time: 711 us; the launch traced here: 707 us
  waiting for transfers between devices  232 us (33%)
  matrix products  158 us (22%)
  other arithmetic  141 us (20%)
  blocking collectives  76.8 us (11%)
  local copies, waits for them, and re-layouts  54.8 us (8%)
  starting transfers between devices  26.9 us (4%)
  between operations  14.5 us (2%)
    psum x1, waiting for transfers between devices, body(): lax.psum((finished[1], finished[2], finished[3], mlp_terms[0], mlp_terms[...  161 us
    psum x1, blocking collectives, body(): lax.psum((finished[1], finished[2], finished[3], mlp_terms[0], mlp_terms[...  76.8 us
    all_to_all x4, waiting for transfers between devices, swap_slots(): lax.all_to_all(blocks, ('outer', 'link'), split_axis=0, concat_axis=0, ti...  71.6 us
    dot_general x48, matrix products, gate_terms(): jnp.dot(hop_input, input_weight, preferred_element_type=jnp.float32)  31.8 us
    dot_general x48, matrix products, gate_terms(): jnp.dot(state_now.astype(jnp.bfloat16), hidden_weight, preferred_element_...  31.7 us
    dot_general x24, matrix products, back_step(): jnp.dot(state_now.astype(jnp.bfloat16).T, hid_bf, preferred_element_type=...  31 us
    dot_general x24, matrix products, back_step(): jnp.dot(hop_input.T, in_bf, preferred_element_type=jnp.float32)  29.4 us
    all_to_all x4, starting transfers between devices, swap_slots(): lax.all_to_all(blocks, ('outer', 'link'), split_axis=0, concat_axis=0, ti...  26.7 us
  transfers between devices with their start and end apart: 5, of which 4 were waited for; matrix products, arithmetic and copies ran while one was open for 6% of the time, Pallas kernels for 0%

commit v1 on v0

--- a/solution.py
+++ b/solution.py
@@ -229,16 +229,19 @@
         num_segments=link_count,
     )
     summed = lax.psum(
-        (
-            finished[1],
-            finished[2],
-            finished[3],
-            mlp_terms[0],
-            mlp_terms[1],
-            mlp_terms[2],
-            mlp_terms[3],
+        lax.psum(
+            (
+                finished[1],
+                finished[2],
+                finished[3],
+                mlp_terms[0],
+                mlp_terms[1],
+                mlp_terms[2],
+                mlp_terms[3],
+            ),
+            ("outer", "link"),
         ),
-        ("replica", "outer", "link"),
+        "replica",
     )
     device_count = lax.axis_size("replica") * lax.axis_size("outer") * lax.axis_size("link")
     grad_scale = float(device_count * link_count) ** (-0.5)

time: 711 us -> 699 us (0.983)
  waiting for transfers between devices: 232 us -> 211 us
    psum x1, waiting for transfers between devices: 161 us -> 139 us  [body(): lax.psum((finished[1], finished[2], finished[3], mlp_terms[0], mlp_terms[...]
    psum x0 -> x1, blocking collectives: none -> 10.2 us  [body(): lax.psum(lax.psum((finished[1], finished[2], finished[3], mlp_terms[0], m...]
  transfers between devices with their start and end apart: 5 -> 6, of which waited for: 4 -> 4; matrix products, arithmetic and copies ran while one was open for 6% -> 7% of each run, Pallas kernels for 0% -> 0%
where the time goes in v1:
time: 699 us; the launch traced here: 692 us
  waiting for transfers between devices  211 us (30%)
  matrix products  158 us (23%)
  other arithmetic  141 us (20%)
  blocking collectives  83.6 us (12%)
  local copies, waits for them, and re-layouts  54 us (8%)
  starting transfers between devices  27 us (4%)
  between operations  14.5 us (2%)
    psum x1, waiting for transfers between devices, body(): lax.psum((finished[1], finished[2], finished[3], mlp_terms[0], mlp_terms[...  139 us
    psum x1, blocking collectives, body(): lax.psum((finished[1], finished[2], finished[3], mlp_terms[0], mlp_terms[...  73.4 us
    all_to_all x4, waiting for transfers between devices, swap_slots(): lax.all_to_all(blocks, ('outer', 'link'), split_axis=0, concat_axis=0, ti...  71.7 us
    dot_general x48, matrix products, gate_terms(): jnp.dot(hop_input, input_weight, preferred_element_type=jnp.float32)  31.8 us
    dot_general x48, matrix products, gate_terms(): jnp.dot(state_now.astype(jnp.bfloat16), hidden_weight, preferred_element_...  31.7 us
    dot_general x24, matrix products, back_step(): jnp.dot(state_now.astype(jnp.bfloat16).T, hid_bf, preferred_element_type=...  31 us
    dot_general x24, matrix products, back_step(): jnp.dot(hop_input.T, in_bf, preferred_element_type=jnp.float32)  29.4 us
    all_to_all x4, starting transfers between devices, swap_slots(): lax.all_to_all(blocks, ('outer', 'link'), split_axis=0, concat_axis=0, ti...  26.7 us
  transfers between devices with their start and end apart: 6, of which 4 were waited for; matrix products, arithmetic and copies ran while one was open for 7% of the time, Pallas kernels for 0%

profile of v1, /device:TPU:2, one launch (start us, length us, event | category | flops | bytes accessed | tf_op | source)
XLA Modules:
  0.0 692.0 jit_solution(12242869880465089097)
XLA Ops:
  8.8 7.6 %gather_fusion = bf16[2048,256]{1,0:T(8,128)(2,1)S(1)} fusion(bf16[512,256]{1,0:T(8,128)(2,1)} %bitcast.135, s32[2048]{0:T(1024)S(1)} %broadcast_clamp_fusion), kind=kCustom, calls=%fused_computation.clone | custom fusion | bytes 2105344 | tf_op jit(solution)/shard_map/jit(_take)/gather | solution.py:187
  17.7 11.5 %all-to-all-start = ((bf16[32,64,256]{2,1,0:T(8,128)(2,1)}), bf16[32,64,256]{2,1,0:T(8,128)(2,1)S(1)}, u32[]{:S(2)}, u32[]{:S(2)}) async-start(bf16[32,64,256]{2,1,0:T(8,128)(2,1)} %broadcast_select_fusion.2), calls=%async_computation | async-start | bytes 2097152 | tf_op jit(solution)/shard_map/all_to_all | solution.py:155
  29.9 27.9 %all-to-all-done = bf16[32,64,256]{2,1,0:T(8,128)(2,1)S(1)} async-done(((bf16[32,64,256]{2,1,0:T(8,128)(2,1)}), bf16[32,64,256]{2,1,0:T(8,128)(2,1)S(1)}, u32[]{:S(2)}, u32[]{:S(2)}) %all-to-all-start) | async-done | bytes 1048608 | tf_op jit(solution)/shard_map/all_to_all | solution.py:155
  57.8 13.0 %gather_fusion.1 = bf16[3072,256]{1,0:T(8,128)(2,1)} fusion(bf16[2048,256]{1,0:T(8,128)(2,1)S(1)} %bitcast.137, s32[3072]{0:T(1024)S(1)} %bitcast_clamp_fusion), kind=kCustom, calls=%fused_computation.1.clone | custom fusion | bytes 3158016 | tf_op jit(solution)/shard_map/jit(_take)/gather | solution.py:188
  74.6 29.4 %while.35 = (s32[]{:T(128)}, f32[128,256]{1,0:T(8,128)S(1)}, f32[24,128,256]{2,1,0:T(8,128)}, f32[24,128]{1,0:T(8,128)S(1)}, bf16[24,128,256]{2,1,0:T(8,128)(2,1...) while((s32[]{:T(128)}, f32[128,256]{1,0:T(8,128)S(1)}, ...), condition=%wide.region_1.4_spmd, body=%wide.region_0.3_spmd.sunk | while | flops 101253248 | bytes 2954097 | solution.py:36
  104.0 4.6 broadcast_multiply_fusion
  108.5 17.9 %scatter_custom_fusion = f32[2048,256]{1,0:T(8,128)S(1)} fusion(s32[3072]{0:T(1024)S(1)} %bitcast.155, f32[3072,256]{1,0:T(8,128)} %bitcast.148, f32[]{:T(128)} %constant.108.clone.1), kind=kCustom, calls=%fused_computation.102 | custom fusion | flops 786432 | bytes 2097664 | tf_op jit(solution)/shard_map/scatter-add | solution.py:190
  127.6 5.2 all-to-all-start.1
  135.5 25.6 %all-to-all-done.1 = bf16[32,64,256]{2,1,0:T(8,128)(2,1)S(1)} async-done(((bf16[32,64,256]{2,1,0:T(8,128)(2,1)}), bf16[32,64,256]{2,1,0:T(8,128)(2,1)S(1)}, u32[]{:S(2)}, u32[]{:S(2)}) %all-to-all-start.1) | async-done | bytes 1048608 | tf_op jit(solution)/shard_map/all_to_all | solution.py:155
  161.1 11.9 %scatter_custom_fusion.1 = f32[512,256]{1,0:T(8,128)S(1)} fusion(s32[2048]{0:T(1024)} %reshape.174, bf16[2048,256]{1,0:T(8,128)(2,1)S(1)} %bitcast.146, f32[]{:T(128)} %constant.108.clone.1), kind=kCustom, calls=%fused_computation.84 | custom fusion | flops 1048576 | bytes 1573376 | tf_op jit(solution)/shard_map/scatter-add | solution.py:196
  177.0 7.5 %gather_fusion.2 = bf16[2048,256]{1,0:T(8,128)(2,1)S(1)} fusion(bf16[512,256]{1,0:T(8,128)(2,1)S(1)} %convolution_convert_fusion, s32[2048]{0:T(1024)S(1)} %broadcast_clamp_fusion), kind=kCustom, calls=%fused_computation.2.clone | custom fusion | bytes 2105344 | tf_op jit(solution)/shard_map/jit(_take)/gather | solution.py:210
  185.7 4.9 all-to-all-start.2
  194.2 2.1 slice.91
  200.7 18.2 %all-to-all-done.2 = bf16[32,64,256]{2,1,0:T(8,128)(2,1)S(1)} async-done(((bf16[32,64,256]{2,1,0:T(8,128)(2,1)}), bf16[32,64,256]{2,1,0:T(8,128)(2,1)S(1)}, u32[]{:S(2)}, u32[]{:S(2)}) %all-to-all-start.2) | async-done | bytes 1048608 | tf_op jit(solution)/shard_map/all_to_all | solution.py:155
  218.9 12.9 %gather_fusion.3 = bf16[3072,256]{1,0:T(8,128)(2,1)} fusion(bf16[2048,256]{1,0:T(8,128)(2,1)S(1)} %bitcast.136, s32[3072]{0:T(1024)S(1)} %copy-done.32), kind=kCustom, calls=%fused_computation.3.clone | custom fusion | bytes 3158016 | tf_op jit(solution)/shard_map/jit(_take)/gather | solution.py:212
  231.9 4.1 convert_multiply_fusion
  238.1 176.1 %while.36 = (s32[]{:T(128)}, f32[128,256]{1,0:T(8,128)S(1)}, f32[256,768]{1,0:T(8,128)S(1)}, f32[256,768]{1,0:T(8,128)S(1)}, f32[768]{0:T(1024)S(1)}, /*index=5*...) while((s32[]{:T(128)}, f32[128,256]{1,0:T(8,128)S(1)}, ...), condition=%wide.region_6.9_spmd.clone, body=%wide.region_4.8_spmd.clone.sunk | while | flops 306152320 | bytes 12996093 | solution.py:108
  415.3 17.9 %scatter_custom_fusion.2 = f32[2048,256]{1,0:T(8,128)S(1)} fusion(s32[3072]{0:T(1024)} %bitcast.154, f32[3072,256]{1,0:T(8,128)} %bitcast.147, f32[]{:T(128)} %constant.108.clone.1), kind=kCustom, calls=%fused_computation.100 | custom fusion | flops 786432 | bytes 2097664 | tf_op jit(solution)/shard_map/scatter-add | solution.py:220
  434.3 5.1 all-to-all-start.3
  439.5 139.5 %all-reduce.7.cloned.1.call-done = (f32[256,768]{1,0:T(8,128)}, f32[256,768]{1,0:T(8,128)}, f32[512,256]{1,0:T(8,128)}, f32[256,256]{1,0:T(8,128)}) async-done(((f32[256,768]{1,0:T(8,128)}, f32[256,768]{1,0:T(8,128)}, f32[512,256]{1,0:T(8,128)}, f32[256,256]{1,0:T(8,128)}), (f32[256,768]{1,0:T(8,128)}, f32[256,768]{1,0:T(8,128)}, f32[512,256]{1,0:T(8,128)}, ...) | async-done | bytes 2359312 | tf_op jit(solution)/shard_map/psum | solution.py:232
  582.0 73.4 %all-reduce = (f32[768]{0:T(1024)S(1)}, f32[256]{0:T(256)S(1)}, f32[256]{0:T(256)S(1)}) all-reduce(f32[768]{0:T(1024)S(1)} %get-tuple-element.357, f32[256]{0:T(256)S(1)} %copy-done.39, f32[256]{0:T(256)S(1)} %fusion.64), channel_id=1, replica_groups=mesh['replica'=8,'outer'=4,'link'=8] {'outer','link'}, use_global_device_ids=true, to_apply=%region_13.16 | all-reduce | flops 1280 | bytes 10240 | tf_op jit(solution)/shard_map/psum | solution.py:232
  655.4 10.2 %all-reduce.2 = (f32[768]{0:T(1024)S(1)}, f32[256]{0:T(256)S(1)}, f32[256]{0:T(256)S(1)}) all-reduce(f32[768]{0:T(1024)S(1)} %get-tuple-element.452, f32[256]{0:T(256)S(1)} %get-tuple-element.453, f32[256]{0:T(256)S(1)} %get-tuple-element.454), channel_id=1, replica_groups=mesh['replica'=8,'outer'=4,'link'=8] {'replica'}, use_global_device_ids=true, to_apply=%region_14.17 | all-reduce | flops 1280 | bytes 10240 | tf_op jit(solution)/shard_map/psum | solution.py:231
  667.4 12.0 %scatter_custom_fusion.3 = f32[512,256]{1,0:T(8,128)S(1)} fusion(f32[512,256]{1,0:T(8,128)S(1)} %convolution_add_fusion.5, s32[2048]{0:T(1024)} %reshape.174, bf16[2048,256]{1,0:T(8,128)(2,1)S(1)} %bitcast.145), kind=kCustom, calls=%fused_computation.82 | custom fusion | flops 1048576 | bytes 1572864 | tf_op jit(solution)/shard_map/scatter-add | solution.py:226
  679.4 2.3 broadcast_multiply_fusion.2
  (563 shorter events, 239.8 us)
Async XLA Ops:
  7.2 166.7 %copy-start = (bf16[256,256]{1,0:T(8,128)(2,1)S(1)}, bf16[256,256]{1,0:T(8,128)(2,1)}, u32[]{:S(2)}) copy-start(bf16[256,256]{1,0:T(8,128)(2,1)} %param.36) | copy-start | bytes 393220
  16.4 12.8 %copy-start.34 = (s32[1,128,24]{1,2,0:T(8,128)S(1)}, s32[1,128,24]{1,2,0:T(8,128)}, u32[]{:S(2)}) copy-start(s32[1,128,24]{1,2,0:T(8,128)} %param.25) | copy-start | bytes 36868
  16.4 12.8 %copy-start.40 = (s32[1,128]{1,0:T(1,128)S(1)}, s32[1,128]{1,0:T(1,128)}, u32[]{:S(2)}) copy-start(s32[1,128]{1,0:T(1,128)} %param.26) | copy-start | bytes 1540
  16.4 12.8 %copy-start.33 = (bf16[1,128,256]{2,1,0:T(8,128)(2,1)S(1)}, bf16[1,128,256]{2,1,0:T(8,128)(2,1)}, u32[]{:S(2)}) copy-start(bf16[1,128,256]{2,1,0:T(8,128)(2,1)} %param.24) | copy-start | bytes 196612
  17.7 40.1 %all-to-all-start = ((bf16[32,64,256]{2,1,0:T(8,128)(2,1)}), bf16[32,64,256]{2,1,0:T(8,128)(2,1)S(1)}, u32[]{:S(2)}, u32[]{:S(2)}) async-start(bf16[32,64,256]{2,1,0:T(8,128)(2,1)} %broadcast_select_fusion.2), calls=%async_computation | async-start | bytes 2097152 | tf_op jit(solution)/shard_map/all_to_all | solution.py:155
  29.2 41.6 %copy-start.31 = (s32[3072]{0:T(1024)}, s32[3072]{0:T(1024)S(1)}, u32[]{:S(2)}) copy-start(s32[3072]{0:T(1024)S(1)} %bitcast_clamp_fusion) | copy-start | bytes 36868
  29.2 41.5 %copy-start.35 = (pred[24,128]{1,0:T(8,128)(4,1)}, pred[24,128]{1,0:T(8,128)(4,1)S(1)}, u32[]{:S(2)}) copy-start(pred[24,128]{1,0:T(8,128)(4,1)S(1)} %get-tuple-element.481) | copy-start | bytes 9220
  126.5 8.8 %copy-start.1 = (bf16[1,512,256]{2,1,0:T(8,128)(2,1)S(1)}, bf16[1,512,256]{2,1,0:T(8,128)(2,1)}, u32[]{:S(2)}) copy-start(bf16[1,512,256]{2,1,0:T(8,128)(2,1)} %param.23) | copy-start | bytes 786436
  126.5 8.8 %copy-start.13 = (bf16[512,256]{1,0:T(8,128)(2,1)S(1)}, bf16[512,256]{1,0:T(8,128)(2,1)}, u32[]{:S(2)}) copy-start(bf16[512,256]{1,0:T(8,128)(2,1)} %param.34) | copy-start | bytes 786436
  127.6 7.1 %copy-start.38 = (s32[1,512]{1,0:T(1,128)S(1)}, s32[1,512]{1,0:T(1,128)}, u32[]{:S(2)}) copy-start(s32[1,512]{1,0:T(1,128)} %param.27) | copy-start | bytes 6148
  127.6 45.4 %copy-start.14 = (bf16[512,256]{1,0:T(8,128)(2,1)S(1)}, bf16[512,256]{1,0:T(8,128)(2,1)}, u32[]{:S(2)}) copy-start(bf16[512,256]{1,0:T(8,128)(2,1)} %param.34) | copy-start | bytes 786436
  127.6 33.5 %all-to-all-start.1 = ((bf16[32,64,256]{2,1,0:T(8,128)(2,1)}), bf16[32,64,256]{2,1,0:T(8,128)(2,1)S(1)}, u32[]{:S(2)}, u32[]{:S(2)}) async-start(bf16[32,64,256]{2,1,0:T(8,128)(2,1)} %bitcast.142), calls=%async_computation.1 | async-start | bytes 2097152 | tf_op jit(solution)/shard_map/all_to_all | solution.py:155
  185.7 33.2 %all-to-all-start.2 = ((bf16[32,64,256]{2,1,0:T(8,128)(2,1)}), bf16[32,64,256]{2,1,0:T(8,128)(2,1)S(1)}, u32[]{:S(2)}, u32[]{:S(2)}) async-start(bf16[32,64,256]{2,1,0:T(8,128)(2,1)} %broadcast_select_fusion.1), calls=%async_computation.2 | async-start | bytes 2097152 | tf_op jit(solution)/shard_map/all_to_all | solution.py:155
  190.6 388.3 %all-reduce.7.cloned.1.call-start = ((), (), s32[]{:S(2)}) async-start(), calls=%async_computation.4 | async-start | bytes 4718592 | tf_op jit(solution)/shard_map/psum | solution.py:232
  198.7 20.2 %copy-start.32 = (s32[3072]{0:T(1024)S(1)}, s32[3072]{0:T(1024)}, u32[]{:S(2)}) copy-start(s32[3072]{0:T(1024)} %copy-done.31) | copy-start | bytes 36868
  218.9 12.9 %copy-start.30 = (f32[24,128]{1,0:T(8,128)S(1)}, f32[24,128]{1,0:T(8,128)}, u32[]{:S(2)}) copy-start(f32[24,128]{1,0:T(8,128)} %copy-done.29) | copy-start | bytes 36868
  218.9 13.0 %copy-start.36 = (pred[24,128]{1,0:T(8,128)(4,1)S(1)}, pred[24,128]{1,0:T(8,128)(4,1)}, u32[]{:S(2)}) copy-start(pred[24,128]{1,0:T(8,128)(4,1)} %copy-done.35) | copy-start | bytes 9220
  414.1 19.1 %copy-start.8 = (f32[128,256]{1,0:T(8,128)}, f32[128,256]{1,0:T(8,128)S(1)}, u32[]{:S(2)}) copy-start(f32[128,256]{1,0:T(8,128)S(1)} %get-tuple-element.354) | copy-start | bytes 393220
  434.3 144.6 %copy-start.17 = (bf16[1,512,256]{2,1,0:T(8,128)(2,1)S(1)}, bf16[1,512,256]{2,1,0:T(8,128)(2,1)}, u32[]{:S(2)}) copy-start(bf16[1,512,256]{2,1,0:T(8,128)(2,1)} %param.29) | copy-start | bytes 786436
  434.3 146.4 %copy-start.21 = (f32[512,256]{1,0:T(8,128)S(1)}, f32[512,256]{1,0:T(8,128)}, u32[]{:S(2)}) copy-start(f32[512,256]{1,0:T(8,128)} %copy-done.19) | copy-start | bytes 1572868
  434.3 146.4 %copy-start.41 = (f32[256]{0:T(256)S(1)}, f32[256]{0:T(256)}, u32[]{:S(2)}) copy-start(f32[256]{0:T(256)} %param.37) | copy-start | bytes 3076
  434.3 233.0 %all-to-all-start.3 = ((bf16[32,64,256]{2,1,0:T(8,128)(2,1)}), bf16[32,64,256]{2,1,0:T(8,128)(2,1)S(1)}, u32[]{:S(2)}, u32[]{:S(2)}) async-start(bf16[32,64,256]{2,1,0:T(8,128)(2,1)} %bitcast.141), calls=%async_computation.3 | async-start | bytes 2097152 | tf_op jit(solution)/shard_map/all_to_all | solution.py:155
  439.4 240.0 %all-reduce.9.cloned.1.call-start = ((), (), s32[]{:S(2)}) async-start(), calls=%async_computation.5 | async-start | bytes 4718592 | tf_op jit(solution)/shard_map/psum | solution.py:231
  679.3 5.8 copy-start.24
  (47 other events, 112.4 us)
Sparse Core Ops, SparseCore 0:
  415.4 163.4 all-reduce.6
  581.5 66.7 all-reduce.8
